TPU v7x, 32 devices: a whole 2x2x4 slice. The times are simulated.
32 devices in a mesh: sect: 4 (over x, core), cell: 8 (over z, y).
Axes of the slice: x: 2, y: 2, z: 4, core: 2. Of those that a mesh axis runs over, the one named last changes fastest.
Arguments:
- atm_fields: bfloat16 [24, 131072], P(None, ('sect', 'cell')), may hold values from -6 to 6
- ocn_state: float32 [8, 262144], P(None, ('sect', 'cell')), may hold values from -6 to 6
- ice_state: float32 [8, 262144], P(None, ('sect', 'cell')), may hold values from -6 to 6
- ice_level: int32 [262144], P(('sect', 'cell')), may hold values from 0 to 8
- lnd_state: float32 [8, 65536], P(None, ('sect', 'cell')), may hold values from -6 to 6
- lnd_level: int32 [65536], P(('sect', 'cell')), may hold values from 1 to 8
- ocn_map: int32 [2048, 2], P(('sect', 'cell')), may hold values from 0 to 1023, as said below
- ocn_local: int32 [2048, 2], P(('sect', 'cell')), may hold values from 0 to 31
- ocn_tiles: bfloat16 [2048, 4, 128, 128], P(('sect', 'cell')), may hold values from -0.25 to 0.25
- lnd_map: int32 [512, 2], P(('sect', 'cell')), may hold values from 0 to 1023, as said below
- lnd_local: int32 [512, 2], P(('sect', 'cell')), may hold values from 0 to 31
- lnd_tiles: bfloat16 [512, 4, 128, 128], P(('sect', 'cell')), may hold values from -0.25 to 0.25
Outputs:
- atm_flux: float32 [8, 131072], P(None, ('sect', 'cell'))
- ocn_flux: float32 [8, 262144], P(None, ('sect', 'cell'))
- lnd_flux: float32 [8, 65536], P(None, ('sect', 'cell'))
Inputs may be any that keep to these rules, and one draw needn't show every extreme that they name: Global atmosphere block indices; the device of block b is b // 32, and devices are numbered sect-major. For the ocn_map rows of one device q's 64 ocean blocks taken together with the lnd_map rows of its 16 land blocks, every named device is (q + t) modulo the device count for some t from -4 to 3; at most 30 of these entries name any one device, and exactly 30 name some device. `lnd_map`: global atmosphere block indices, counted together with ocn_map as stated there.
All inputs are finite; a program needn't handle non-finite values.
Results may differ from a plain program's by a relative error of at most 0.0022.
Values may be sent and summed in bfloat16 or wider, within the bound.
A program may use at most 64 MiB of HBM per device.

v0:
```python
import jax
import jax.numpy as jnp
from jax import lax
from jax.sharding import PartitionSpec as P

ocean_coef = (1.2, 0.9, 1.5, 0.7, 1.1, 1.3, 0.8, 1.0)
ice_coef = (0.5, 1.4, 0.6, 1.2, 0.9, 0.4, 1.6, 0.7)
land_coef = (0.8, 1.1, 0.6, 1.5, 0.7, 1.2, 1.0, 0.5)


def padded(x, sides, width):
    for axis, dim in sides:
        size, length = (lax.axis_size(axis), x.shape[dim])
        up = [(i, (i + 1) % size) for i in range(size)]
        down = [(j, i) for i, j in up]
        last = lax.slice_in_dim(x, length - width, length, axis=dim)
        initial = lax.slice_in_dim(x, 0, width, axis=dim)
        before = lax.ppermute(last, axis, up)
        after = lax.ppermute(initial, axis, down)
        x = jnp.concatenate([before, x, after], axis=dim)
    return x


def bulk_flux(remapped, surface, factors):
    wind_speed = jnp.sqrt(
        1.0 + remapped[:, 0::3] * remapped[:, 0::3] + remapped[:, 1::3] * remapped[:, 1::3]
    )
    weights = jnp.asarray(factors, jnp.float32)[None, :, None]
    return weights * wind_speed * (remapped[:, 2::3] - surface)


def pair_ranks(owner_dev):
    position = jnp.arange(owner_dev.shape[-1])
    earlier = position[None, :] < position[:, None]
    same_owner = (owner_dev[..., :, None] == owner_dev[..., None, :]) & earlier
    return jnp.sum(same_owner.astype(jnp.int32), axis=-1)


def as_blocks(array, count, block_len):
    return array.reshape(array.shape[0], count, block_len).transpose(1, 0, 2)


def per_device(
    atm_fields,
    ocn_state,
    ice_state,
    ice_level,
    lnd_state,
    lnd_level,
    ocn_map,
    ocn_local,
    ocn_tiles,
    lnd_map,
    lnd_local,
    lnd_tiles,
):
    field_count, width_all = atm_fields.shape
    block_len = ocn_tiles.shape[2]
    flux_count = ocn_state.shape[0]
    blocks_here = width_all // block_len
    ocean_blocks = ocn_map.shape[0]
    land_blocks = lnd_map.shape[0]
    remote_count = ocn_map.shape[1]
    cell_count = lax.axis_size("cell")
    my_index = lax.axis_index(("sect", "cell"))
    my_cell = my_index % cell_count
    source = jnp.concatenate([ocn_map.reshape(-1), lnd_map.reshape(-1)])
    pair_count = source.shape[0]
    base_share = (pair_count + cell_count - 1) // cell_count
    capacity = base_share + (base_share + 1) // 2
    owner_dev = source // blocks_here
    pair_rank = pair_ranks(owner_dev)
    row_maps = lax.all_gather(source, "cell", axis=0, tiled=True).reshape(1, cell_count, pair_count)
    near_maps = padded(row_maps, (("sect", 0),), 1)
    near_owner = near_maps // blocks_here
    near_rank = pair_ranks(near_owner)
    match_mask = (near_owner == my_index)[..., None] & (
        near_rank[..., None] == jnp.arange(capacity)[None, None, None, :]
    )
    wanted = jnp.sum(jnp.where(match_mask, (near_maps % blocks_here)[..., None] + 1, 0), axis=2) - 1
    atm_rows = atm_fields.reshape(field_count, blocks_here, block_len).transpose(1, 0, 2)
    flat_rows = atm_rows.reshape(blocks_here, field_count * block_len)
    row_width = field_count * block_len
    term_width = flux_count * block_len
    three_picker = wanted.reshape(-1)[:, None] == jnp.arange(blocks_here)[None, :]
    outgoing = jnp.dot(
        three_picker.astype(jnp.bfloat16), flat_rows, preferred_element_type=jnp.float32
    ).astype(jnp.bfloat16)
    rimmed = padded(outgoing.reshape(3, cell_count * capacity, row_width), (("sect", 0),), 1)
    relayed = rimmed[0] + rimmed[2] + rimmed[4]
    incoming = lax.all_to_all(relayed, "cell", split_axis=0, concat_axis=0, tiled=True)
    wanted_rows = jnp.max(wanted, axis=0).reshape(-1)
    picker = wanted_rows[:, None] == jnp.arange(blocks_here)[None, :]
    slot_of = owner_dev % cell_count * capacity + pair_rank
    slot_count = cell_count * capacity
    pair_data = jnp.take(incoming, slot_of, axis=0)
    ocean_pairs = ocean_blocks * remote_count
    ocean_remote = pair_data[:ocean_pairs].reshape(
        ocean_blocks, remote_count, field_count, block_len
    )
    land_remote = pair_data[ocean_pairs:].reshape(land_blocks, remote_count, field_count, block_len)
    ocean_sources = jnp.concatenate([ocean_remote, jnp.take(atm_rows, ocn_local, axis=0)], axis=1)
    land_sources = jnp.concatenate([land_remote, jnp.take(atm_rows, lnd_local, axis=0)], axis=1)
    ocean_mixed = jnp.einsum(
        "bkfs,bksd->bfd", ocean_sources, ocn_tiles, preferred_element_type=jnp.float32
    )
    land_mixed = jnp.einsum(
        "bkfs,bksd->bfd", land_sources, lnd_tiles, preferred_element_type=jnp.float32
    )
    ice_frac = (ice_level.astype(jnp.float32) / 8.0).reshape(ocean_blocks, 1, block_len)
    ocean_flux = (1.0 - ice_frac) * bulk_flux(
        ocean_mixed, as_blocks(ocn_state, ocean_blocks, block_len), ocean_coef
    )
    ocean_flux = ocean_flux + ice_frac * bulk_flux(
        ocean_mixed, as_blocks(ice_state, ocean_blocks, block_len), ice_coef
    )
    land_frac = (lnd_level.astype(jnp.float32) / 8.0).reshape(land_blocks, 1, block_len)
    land_flux = land_frac * bulk_flux(
        land_mixed, as_blocks(lnd_state, land_blocks, block_len), land_coef
    )
    ocean_terms = jnp.einsum(
        "bfd,bksd->bkfs",
        ocean_flux.astype(jnp.bfloat16),
        ocn_tiles,
        preferred_element_type=jnp.float32,
    )
    land_terms = jnp.einsum(
        "bfd,bksd->bkfs",
        land_flux.astype(jnp.bfloat16),
        lnd_tiles,
        preferred_element_type=jnp.float32,
    )
    remote_terms = jnp.concatenate(
        [
            ocean_terms[:, :remote_count].reshape(-1, term_width),
            land_terms[:, :remote_count].reshape(-1, term_width),
        ],
        axis=0,
    )
    local_terms = jnp.concatenate(
        [
            ocean_terms[:, remote_count:].reshape(-1, term_width),
            land_terms[:, remote_count:].reshape(-1, term_width),
        ],
        axis=0,
    )
    local_targets = jnp.concatenate([ocn_local.reshape(-1), lnd_local.reshape(-1)])
    back_out = jnp.zeros((slot_count, term_width), jnp.float32).at[slot_of].set(remote_terms)
    crossed = lax.all_to_all(back_out, "cell", split_axis=0, concat_axis=0, tiled=True).reshape(
        cell_count, capacity, term_width
    )
    sect_step = (
        jnp.arange(cell_count, dtype=jnp.int32) - my_cell + cell_count // 2 - 1
    ) // cell_count
    stacked = jnp.stack(
        [jnp.where((sect_step == step - 1)[:, None, None], crossed, 0.0) for step in range(3)]
    ).reshape(3, cell_count * capacity, term_width)
    rimmed_back = padded(stacked, (("sect", 0),), 1)
    back_in = rimmed_back[0] + rimmed_back[2] + rimmed_back[4]
    local_picker = (local_targets[None, :] == jnp.arange(blocks_here)[:, None]).astype(jnp.float32)
    summed = jnp.dot(local_picker, local_terms, precision=lax.Precision.HIGHEST)
    summed = summed + jnp.dot(
        picker.astype(jnp.float32).T, back_in, precision=lax.Precision.HIGHEST
    )
    atm_flux = (
        summed.reshape(blocks_here, flux_count, block_len)
        .transpose(1, 0, 2)
        .reshape(flux_count, width_all)
    )
    ocn_flux = ocean_flux.transpose(1, 0, 2).reshape(flux_count, ocean_blocks * block_len)
    lnd_flux = land_flux.transpose(1, 0, 2).reshape(flux_count, land_blocks * block_len)
    return (atm_flux, ocn_flux, lnd_flux)


def solution(mesh):
    in_specs = (
        P(None, ("sect", "cell")),
        P(None, ("sect", "cell")),
        P(None, ("sect", "cell")),
        P(("sect", "cell")),
        P(None, ("sect", "cell")),
        P(("sect", "cell")),
        P(("sect", "cell"), None),
        P(("sect", "cell"), None),
        P(("sect", "cell"), None, None, None),
        P(("sect", "cell"), None),
        P(("sect", "cell"), None),
        P(("sect", "cell"), None, None, None),
    )
    out_specs = (P(None, ("sect", "cell")), P(None, ("sect", "cell")), P(None, ("sect", "cell")))
    return jax.shard_map(
        per_device, mesh=mesh, in_specs=in_specs, out_specs=out_specs, check_vma=False
    )
```

profile of v0, /device:TPU:0, one launch (start us, length us, event | category | flops | bytes accessed | tf_op | source)
XLA Modules:
  0.0 208.7 jit_solution(8948492196828670128)
XLA Ops:
  2.6 1.2 dynamic-slice
  4.8 13.2 %all-reduce = s32[1280]{0:T(1024)S(1)} all-reduce(s32[1280]{0:T(1024)S(1)} %dynamic-update-slice), channel_id=1, replica_groups=mesh['sect'=4,'cell'=8] {'cell'}, use_global_device_ids=true, to_apply=%add | all-reduce | flops 1280 | bytes 10240
  18.1 1.7 collective-permute-start.1
  21.3 1.7 convert_reduce_fusion
  23.0 1.6 select_reduce_fusion
  25.4 1.4 convolution_convert_fusion
  26.8 2.1 %fusion.51 = (bf16[240,3072]{1,0:T(8,128)(2,1)}, bf16[1,240,3072]{2,1,0:T(8,128)(2,1)}, bf16[1,240,3072]{2,1,0:T(8,128)(2,1)}) fusion(bf16[720,3072]{1,0:T(8,128)(2,1)S(1)} %convolution_convert_fusion), kind=kLoop, calls=%fused_computation.137 | loop fusion | bytes 8847360 | tf_op jit(solution)/shard_map/slice | solution.py:90
  28.9 1.6 collective-permute-start.2
  31.5 2.5 %squeeze.19 = bf16[8,30,3072]{2,1,0:T(8,128)(2,1)} reshape(bf16[240,3072]{1,0:T(8,128)(2,1)} %get-tuple-element.5) | data formatting | bytes 2949120 | tf_op jit(solution)/shard_map/squeeze | solution.py:90
  34.0 28.1 %collective-permute-done.2 = bf16[1,240,3072]{2,1,0:T(8,128)(2,1)} collective-permute-done((bf16[1,240,3072]{2,1,0:T(8,128)(2,1)}, bf16[1,240,3072]{2,1,0:T(8,128)(2,1)}, u32[]{:S(2)}, u32[]{:S(2)}) %collective-permute-start.2) | collective-permute-done | bytes 1474592 | tf_op jit(solution)/shard_map/ppermute | solution.py:18
  62.1 2.5 %squeeze.18 = bf16[8,30,3072]{2,1,0:T(8,128)(2,1)} reshape(bf16[1,240,3072]{2,1,0:T(8,128)(2,1)} %collective-permute-done.2) | data formatting | bytes 2949120 | tf_op jit(solution)/shard_map/squeeze | solution.py:90
  64.5 2.5 %squeeze.20 = bf16[8,30,3072]{2,1,0:T(8,128)(2,1)} reshape(bf16[1,240,3072]{2,1,0:T(8,128)(2,1)} %collective-permute-done.3) | data formatting | bytes 2949120 | tf_op jit(solution)/shard_map/squeeze | solution.py:90
  67.0 3.7 %add_add_fusion = bf16[8,30,3072]{2,1,0:T(8,128)(2,1)} fusion(bf16[8,30,3072]{2,1,0:T(8,128)(2,1)} %squeeze.20, bf16[8,30,3072]{2,1,0:T(8,128)(2,1)} %squeeze.18, bf16[8,30,3072]{2,1,0:T(8,128)(2,1)} %squeeze.19), kind=kLoop, calls=%fused_computation.10 | loop fusion | flops 1474560 | bytes 5898240 | tf_op jit(solution)/shard_map/add | solution.py:90
  70.8 4.5 %all-to-all-start = ((bf16[8,30,3072]{2,1,0:T(8,128)(2,1)}), bf16[8,30,3072]{2,1,0:T(8,128)(2,1)}, u32[]{:S(2)}, u32[]{:S(2)}) async-start(bf16[8,30,3072]{2,1,0:T(8,128)(2,1)} %add_add_fusion), calls=%async_computation | async-start | bytes 3145728 | tf_op jit(solution)/shard_map/all_to_all | solution.py:91
  78.8 33.8 %all-to-all-done = bf16[8,30,3072]{2,1,0:T(8,128)(2,1)} async-done(((bf16[8,30,3072]{2,1,0:T(8,128)(2,1)}), bf16[8,30,3072]{2,1,0:T(8,128)(2,1)}, u32[]{:S(2)}, u32[]{:S(2)}) %all-to-all-start) | async-done | bytes 1474592 | tf_op jit(solution)/shard_map/all_to_all | solution.py:91
  112.6 2.4 %all_to_all.13 = bf16[240,3072]{1,0:T(8,128)(2,1)} reshape(bf16[8,30,3072]{2,1,0:T(8,128)(2,1)} %all-to-all-done) | data formatting | bytes 2949120 | tf_op jit(solution)/shard_map/all_to_all | solution.py:91
  115.0 4.7 %gather_fusion = bf16[160,3072]{1,0:T(8,128)(2,1)} fusion(bf16[240,3072]{1,0:T(8,128)(2,1)} %all_to_all.13, s32[1024]{0:T(1024)S(1)} %pad_clamp_fusion.2), kind=kCustom, calls=%fused_computation | custom fusion | bytes 1966720 | tf_op jit(solution)/shard_map/jit(_take)/gather | solution.py:96
  119.8 1.4 broadcast_select_fusion
  122.3 5.6 %fusion.4 = f32[64,24,128]{2,1,0:T(8,128)} fusion(bf16[64,4,128,128]{3,2,1,0:T(8,128)(2,1)} %param.23, bf16[64,2,24,128]{3,2,1,0:T(8,128)(2,1)S(1)} %copy-done.3, bf16[64,2,24,128]{3,2,1,0:T(8,128)(2,1)S(1)} %bitcast.130), kind=kOutput, calls=%fused_computation.14 | convolution fusion | flops 202113024 | bytes 10747904 | tf_op jit(solution)/shard_map/bkfs,bksd->bfd/dot_general | solution.py:104
  127.9 2.6 %slice.77 = f32[64,8,128]{2,1,0:T(8,128)} slice(f32[64,24,128]{2,1,0:T(8,128)} %fusion.4), slice={[0:64:1], [0:24:3], [0:128:1]} | slice | bytes 524288 | tf_op jit(solution)/shard_map/slice | solution.py:26
  130.5 2.6 %slice.78 = f32[64,8,128]{2,1,0:T(8,128)} slice(f32[64,24,128]{2,1,0:T(8,128)} %fusion.4), slice={[0:64:1], [1:24:3], [0:128:1]} | slice | bytes 524288 | tf_op jit(solution)/shard_map/slice | solution.py:26
  133.0 2.6 %slice.79 = f32[64,8,128]{2,1,0:T(8,128)} slice(f32[64,24,128]{2,1,0:T(8,128)} %fusion.4), slice={[0:64:1], [2:24:3], [0:128:1]} | slice | bytes 524288 | tf_op jit(solution)/shard_map/slice | solution.py:29
  136.8 1.2 fusion.23
  138.0 5.7 %convolution_bitcast_fusion = f32[64,4,8,128]{3,2,1,0:T(8,128)S(1)} fusion(bf16[64,4,128,128]{3,2,1,0:T(8,128)(2,1)} %param.23, f32[64,8,128]{2,1,0:T(8,128)S(1)} %fusion.23), kind=kOutput, calls=%fused_computation.13 | convolution fusion | flops 67174400 | bytes 9699328 | tf_op jit(solution)/shard_map/bfd,bksd->bkfs/dot_general | solution.py:121
  146.4 1.9 scatter_custom_fusion
  149.4 3.6 %all-to-all-start.1 = ((f32[8,30,1024]{2,1,0:T(8,128)}), f32[8,30,1024]{2,1,0:T(8,128)S(1)}, u32[]{:S(2)}, u32[]{:S(2)}) async-start(f32[8,30,1024]{2,1,0:T(8,128)} %all_to_all.14), calls=%async_computation.1 | async-start | bytes 2097152 | tf_op jit(solution)/shard_map/all_to_all | solution.py:149
  153.1 25.9 %all-to-all-done.1 = f32[8,30,1024]{2,1,0:T(8,128)S(1)} async-done(((f32[8,30,1024]{2,1,0:T(8,128)}), f32[8,30,1024]{2,1,0:T(8,128)S(1)}, u32[]{:S(2)}, u32[]{:S(2)}) %all-to-all-start.1) | async-done | bytes 983072 | tf_op jit(solution)/shard_map/all_to_all | solution.py:149
  179.0 1.8 broadcast_select_fusion.4
  180.8 2.4 %slice.88 = f32[1,240,1024]{2,1,0:T(8,128)} reshape(f32[8,30,1024]{2,1,0:T(8,128)} %get-tuple-element.8) | data formatting | bytes 1966080 | tf_op jit(solution)/shard_map/slice | solution.py:16
  184.3 1.7 collective-permute-start.5
  189.2 16.5 %collective-permute-done.4 = f32[1,240,1024]{2,1,0:T(8,128)} collective-permute-done((f32[1,240,1024]{2,1,0:T(8,128)}, f32[1,240,1024]{2,1,0:T(8,128)}, u32[]{:S(2)}, u32[]{:S(2)}) %collective-permute-start.4) | collective-permute-done | bytes 983072 | tf_op jit(solution)/shard_map/ppermute | solution.py:18
  205.7 2.4 %fusion.7 = f32[4,8,8,128]{3,1,2,0:T(8,128)S(1)} fusion(f32[32,1024]{1,0:T(8,128)S(1)} %fusion.9, f32[1,240,1024]{2,1,0:T(8,128)} %collective-permute-done.5, f32[240,1024]{1,0:T(8,128)} %squeeze.22, f32[1,240,1024]{2,1,0:T(8,128)} %collective-permute-done.4, s32[240]{0:T(256)S(1)} %eq.134), kind=kOutput, calls=%fused_computation.18 | convolution fusion | flops 94903808 | bytes 3212224 | tf_op jit(solution)/shard_map/dot_general | solution.py:162
  (127 shorter events, 19.7 us)
Async XLA Ops:
  0.6 135.1 %copy-start = (bf16[16,4,128,128]{3,2,1,0:T(8,128)(2,1)S(1)}, bf16[16,4,128,128]{3,2,1,0:T(8,128)(2,1)}, u32[]{:S(2)}) copy-start(bf16[16,4,128,128]{3,2,1,0:T(8,128)(2,1)} %param.26) | copy-start | bytes 6291460
  18.1 3.1 %collective-permute-start = (s32[1,8,160]{2,1,0:T(8,128)S(1)}, s32[1,8,160]{2,1,0:T(8,128)S(1)}, u32[]{:S(2)}, u32[]{:S(2)}) collective-permute-start(s32[1,8,160]{2,1,0:T(8,128)S(1)} %reshape.781), channel_id=1, source_target_pairs={{0,8},{8,16},{16,24},{24,0},{1,9},{9,17},{17,25},{25,1},{2,10},{10... | collective-permute-start | bytes 15368 | tf_op jit(solution)/shard_map/ppermute | solution.py:18
  18.1 3.1 %collective-permute-start.1 = (s32[1,8,160]{2,1,0:T(8,128)S(1)}, s32[1,8,160]{2,1,0:T(8,128)S(1)}, u32[]{:S(2)}, u32[]{:S(2)}) collective-permute-start(s32[1,8,160]{2,1,0:T(8,128)S(1)} %reshape.781), channel_id=1, source_target_pairs={{8,0},{16,8},{24,16},{0,24},{9,1},{17,9},{25,17},{1,25},{10,2},{18... | collective-permute-start | bytes 15368 | tf_op jit(solution)/shard_map/ppermute | solution.py:19
  26.8 4.1 %copy-start.14 = (s32[64,2]{0,1:T(2,128)S(1)}, s32[64,2]{0,1:T(2,128)}, u32[]{:S(2)}) copy-start(s32[64,2]{0,1:T(2,128)} %param.22) | copy-start | bytes 1540
  26.8 4.4 %copy-start.16 = (s32[16,2]{0,1:T(2,128)S(1)}, s32[16,2]{0,1:T(2,128)}, u32[]{:S(2)}) copy-start(s32[16,2]{0,1:T(2,128)} %param.25) | copy-start | bytes 388
  28.9 33.1 %collective-permute-start.2 = (bf16[1,240,3072]{2,1,0:T(8,128)(2,1)}, bf16[1,240,3072]{2,1,0:T(8,128)(2,1)}, u32[]{:S(2)}, u32[]{:S(2)}) collective-permute-start(bf16[1,240,3072]{2,1,0:T(8,128)(2,1)} %get-tuple-element.7), channel_id=1, source_target_pairs={{0,8},{8,16},{16,24},{24,0},{1,9},{9,17},{17,25},{25,1},{2,10},{10... | collective-permute-start | bytes 4423688 | tf_op jit(solution)/shard_map/ppermute | solution.py:18
  30.5 34.0 %collective-permute-start.3 = (bf16[1,240,3072]{2,1,0:T(8,128)(2,1)}, bf16[1,240,3072]{2,1,0:T(8,128)(2,1)}, u32[]{:S(2)}, u32[]{:S(2)}) collective-permute-start(bf16[1,240,3072]{2,1,0:T(8,128)(2,1)} %get-tuple-element.6), channel_id=1, source_target_pairs={{8,0},{16,8},{24,16},{0,24},{9,1},{17,9},{25,17},{1,25},{10,2},{18... | collective-permute-start | bytes 4423688 | tf_op jit(solution)/shard_map/ppermute | solution.py:19
  70.8 41.8 %all-to-all-start = ((bf16[8,30,3072]{2,1,0:T(8,128)(2,1)}), bf16[8,30,3072]{2,1,0:T(8,128)(2,1)}, u32[]{:S(2)}, u32[]{:S(2)}) async-start(bf16[8,30,3072]{2,1,0:T(8,128)(2,1)} %add_add_fusion), calls=%async_computation | async-start | bytes 3145728 | tf_op jit(solution)/shard_map/all_to_all | solution.py:91
  75.2 2.3 %copy-start.12 = (s32[2048]{0:T(1024)S(1)}, s32[2048]{0:T(1024)}, u32[]{:S(2)}) copy-start(s32[2048]{0:T(1024)} %param.20) | copy-start | bytes 24580
  75.3 2.3 %copy-start.9 = (s32[8192]{0:T(1024)S(1)}, s32[8192]{0:T(1024)}, u32[]{:S(2)}) copy-start(s32[8192]{0:T(1024)} %param.18) | copy-start | bytes 98308
  77.0 0.6 copy-start.13
  115.0 4.7 %copy-start.18 = (pred[160]{0:T(512)(128)(4,1)S(1)}, pred[160]{0:T(512)(128)(4,1)}, u32[]{:S(2)}) copy-start(pred[160]{0:T(512)(128)(4,1)} %compare_and_fusion.2) | copy-start | bytes 484
  121.1 1.1 copy-start.3
  135.7 1.0 copy-start.5
  135.7 1.0 copy-start.6
  135.7 1.1 copy-start.7
  135.7 1.1 copy-start.20
  135.7 1.1 copy-start.21
  138.0 5.7 %copy-start.4 = (f32[64,8,128]{2,1,0:T(8,128)}, f32[64,8,128]{2,1,0:T(8,128)S(1)}, u32[]{:S(2)}) copy-start(f32[64,8,128]{2,1,0:T(8,128)S(1)} %fusion.23) | copy-start | bytes 786436
  143.7 1.8 copy-start.10
  143.7 1.8 copy-start.19
  145.7 0.7 copy-start.8
  149.4 29.6 %all-to-all-start.1 = ((f32[8,30,1024]{2,1,0:T(8,128)}), f32[8,30,1024]{2,1,0:T(8,128)S(1)}, u32[]{:S(2)}, u32[]{:S(2)}) async-start(f32[8,30,1024]{2,1,0:T(8,128)} %all_to_all.14), calls=%async_computation.1 | async-start | bytes 2097152 | tf_op jit(solution)/shard_map/all_to_all | solution.py:149
  180.8 2.4 %copy-start.2 = (f32[8,30,1024]{2,1,0:T(8,128)S(1)}, f32[8,30,1024]{2,1,0:T(8,128)}, u32[]{:S(2)}) copy-start(f32[8,30,1024]{2,1,0:T(8,128)} %get-tuple-element.9) | copy-start | bytes 2949124
  180.8 5.2 %copy-start.15 = (s32[64,2]{0,1:T(2,128)S(1)}, s32[64,2]{0,1:T(2,128)}, u32[]{:S(2)}) copy-start(s32[64,2]{0,1:T(2,128)} %param.22) | copy-start | bytes 1540
  180.8 5.3 %copy-start.17 = (s32[16,2]{0,1:T(2,128)S(1)}, s32[16,2]{0,1:T(2,128)}, u32[]{:S(2)}) copy-start(s32[16,2]{0,1:T(2,128)} %param.25) | copy-start | bytes 388
  180.8 5.6 %copy-start.11 = (s32[8,30]{1,0:T(8,128)S(1)}, s32[8,30]{1,0:T(8,128)}, u32[]{:S(2)}) copy-start(s32[8,30]{1,0:T(8,128)} %get-tuple-element.17) | copy-start | bytes 2884
  183.2 22.5 %collective-permute-start.4 = (f32[1,240,1024]{2,1,0:T(8,128)}, f32[1,240,1024]{2,1,0:T(8,128)}, u32[]{:S(2)}, u32[]{:S(2)}) collective-permute-start(f32[1,240,1024]{2,1,0:T(8,128)} %slice.88), channel_id=1, source_target_pairs={{0,8},{8,16},{16,24},{24,0},{1,9},{9,17},{17,25},{25,1},{2,10},{10... | collective-permute-start | bytes 2949128 | tf_op jit(solution)/shard_map/ppermute | solution.py:18
  184.3 3.8 %copy-start.1 = (f32[8,30,1024]{2,1,0:T(8,128)S(1)}, f32[8,30,1024]{2,1,0:T(8,128)}, u32[]{:S(2)}) copy-start(f32[8,30,1024]{2,1,0:T(8,128)} %get-tuple-element.10) | copy-start | bytes 2949124
  184.3 21.4 %collective-permute-start.5 = (f32[1,240,1024]{2,1,0:T(8,128)}, f32[1,240,1024]{2,1,0:T(8,128)}, u32[]{:S(2)}, u32[]{:S(2)}) collective-permute-start(f32[1,240,1024]{2,1,0:T(8,128)} %slice.89), channel_id=1, source_target_pairs={{8,0},{16,8},{24,16},{0,24},{9,1},{17,9},{25,17},{1,25},{10,2},{18... | collective-permute-start | bytes 2949128 | tf_op jit(solution)/shard_map/ppermute | solution.py:19
where the time goes:
time: 211 us; the launch traced here: 209 us
  waiting for transfers between devices  105 us (50%)
  local copies, waits for them, and re-layouts  43 us (20%)
  matrix products  16.5 us (8%)
  other arithmetic  16.2 us (8%)
  starting transfers between devices  13.3 us (6%)
  blocking collectives  13.2 us (6%)
    ppermute x3, waiting for transfers between devices, padded(): before = lax.ppermute(last, axis, up)  44.9 us
    all_to_all x1, waiting for transfers between devices, per_device(): lax.all_to_all(relayed, 'cell', split_axis=0, concat_axis=0, tiled=True)  33.8 us
    all_to_all x1, waiting for transfers between devices, per_device(): lax.all_to_all(back_out, 'cell', split_axis=0, concat_axis=0, tiled=True)  25.9 us
    unnamed x1, blocking collectives  13.2 us
    unnamed x64, local copies, waits for them, and re-layouts  7.97 us
    squeeze x3, local copies, waits for them, and re-layouts, per_device(): relayed = rimmed[0] + rimmed[2] + rimmed[4]  7.43 us
    dot_general x1, matrix products, per_device(): jnp.einsum('bfd,bksd->bkfs', ocean_flux.astype(jnp.bfloat16), ocn_tiles,...  5.73 us
    dot_general x1, matrix products, per_device(): jnp.einsum('bkfs,bksd->bfd', ocean_sources, ocn_tiles, preferred_element_...  5.63 us
  transfers between devices with their start and end apart: 8, of which 5 were waited for; matrix products, arithmetic and copies ran while one was open for 7% of the time, Pallas kernels for 0%

commit v1 on v0

v1 whole, which is shorter than its diff:
```python
import functools

import jax
import jax.numpy as jnp
from jax import lax
from jax.experimental import pallas as pl
from jax.experimental.pallas import tpu as pltpu
from jax.sharding import PartitionSpec as P

ocean_coef = (1.2, 0.9, 1.5, 0.7, 1.1, 1.3, 0.8, 1.0)
ice_coef = (0.5, 1.4, 0.6, 1.2, 0.9, 0.4, 1.6, 0.7)
land_coef = (0.8, 1.1, 0.6, 1.5, 0.7, 1.2, 1.0, 0.5)

GROUP = 8


def coef_column(coef, width):
    row = lax.broadcasted_iota(jnp.int32, (len(coef), width), 0)
    out = jnp.full((len(coef), width), coef[0], jnp.float32)
    for j in range(1, len(coef)):
        out = jnp.where(row == j, coef[j], out)
    return out


def coupler_kernel(
    sizes,
    pick,
    target,
    atm,
    ocn_state,
    ice_state,
    ice_level,
    lnd_state,
    lnd_level,
    ocn_tiles,
    lnd_tiles,
    atm_out,
    ocn_out,
    lnd_out,
    own,
    held,
    tiles,
    so,
    si,
    li,
    sl,
    ll,
    mix,
    terms,
    ocn_v,
    lnd_v,
    outbox,
    inbox,
    own_sum,
    final,
    own_sem,
    keep_sem,
    state_sem,
    tile_sem,
    out_sem,
    send_sem,
    recv_sem,
    back_send,
    back_recv,
):
    sects, cells, ocean_blocks, land_blocks, blocks_here, block, pieces = sizes
    count = sects * cells
    half = cells // 2
    blocks = ocean_blocks + land_blocks
    me = lax.axis_index("sect") * cells + lax.axis_index("cell")
    parity = lax.rem(me, 2)
    delta = 1 - 2 * parity

    def device(number):
        number = lax.rem(number + 2 * count, count)
        return {"sect": lax.div(number, cells), "cell": lax.rem(number, cells)}

    own_copies = []
    for b in range(blocks_here):
        src = atm.at[:, b * block : (b + 1) * block]
        copy = pltpu.make_async_copy(src, own.at[b], own_sem.at[b])
        copy.start()
        own_copies.append(copy)
    tile_copies = []
    for g in range(blocks // GROUP):
        first = g * GROUP
        if first < ocean_blocks:
            src = ocn_tiles.at[pl.ds(first, GROUP)]
        else:
            src = lnd_tiles.at[pl.ds(first - ocean_blocks, GROUP)]
        copy = pltpu.make_async_copy(src, tiles.at[pl.ds(first, GROUP)], tile_sem.at[g])
        copy.start()
        tile_copies.append(copy)
    state_copies = [
        pltpu.make_async_copy(src, dst, state_sem.at[i])
        for i, (src, dst) in enumerate(
            ((ocn_state, so), (ice_state, si), (ice_level, li), (lnd_state, sl), (lnd_level, ll))
        )
    ]
    for copy in state_copies:
        copy.start()

    barrier = pltpu.get_barrier_semaphore()
    greet = [d for d in range(-half, half + 1) if d != 0] + [cells - 1, 1 - cells]
    for d in greet:
        pl.semaphore_signal(
            barrier, inc=1, device_id=device(me + d), device_id_type=pl.DeviceIdType.MESH
        )
    pl.semaphore_wait(barrier, len(greet))
    for copy in own_copies:
        copy.wait()
    keep_copy = pltpu.make_async_copy(own, held.at[pl.ds(half * blocks_here, blocks_here)], keep_sem)
    keep_copy.start()

    width = blocks_here // pieces
    evens = sorted((d for d in range(1 - half, half + 1) if d % 2 == 0 and d != 0), key=lambda d: abs(d))

    def push(slot_here, slot_there, peer, piece, sem):
        here = pl.ds(slot_here * blocks_here + piece * width, width)
        there = pl.ds(slot_there * blocks_here + piece * width, width)
        src = own.at[pl.ds(piece * width, width)] if slot_here == half else held.at[here]
        return pltpu.make_async_remote_copy(
            src_ref=src,
            dst_ref=held.at[there],
            send_sem=send_sem.at[sem, piece],
            recv_sem=recv_sem.at[slot_there, piece],
            device_id=device(peer),
            device_id_type=pl.DeviceIdType.MESH,
        )

    def relay(d, piece, sem):
        moved = d + delta
        wrap = jnp.where(moved == half + 1, cells, 0)
        slot = half - moved + wrap
        return push(half - d, slot, me + delta - wrap, piece, sem)

    sends = []
    for piece in range(pieces):
        for i, d in enumerate(evens):
            sends.append(push(half, half - d, me + d, piece, i))
            sends[-1].start()
        sends.append(relay(0, piece, len(evens)))
        sends[-1].start()

    def source(d, k):
        return held[pick[4 * d + k]]

    def product(d, k):
        lhs = jnp.concatenate([source(d, k), source(d, k + 1)], axis=1)
        rhs = tiles[d, k : k + 2].reshape(2 * block, block)
        return jnp.dot(lhs, rhs, preferred_element_type=jnp.float32)

    def local_source(d, k):
        return own[pick[4 * d + k]]

    def local_group(g):
        for u in range(GROUP):
            d = g * GROUP + u
            lhs = jnp.concatenate([local_source(d, 2), local_source(d, 3)], axis=1)
            rhs = tiles[d, 2:4].reshape(2 * block, block)
            row = pl.multiple_of(d * 24, 24)
            mix[pl.ds(row, 24), :] = jnp.dot(lhs, rhs, preferred_element_type=jnp.float32)

    relays = [(piece, i, d) for piece in range(pieces) for i, d in enumerate(evens)]

    def do_relay(piece, i, d):
        push(half, half - d, me + 1, piece, i).wait_recv()
        sends.append(relay(d, piece, len(evens) + 1 + i))
        sends[-1].start()

    groups = blocks // GROUP
    for g in range(groups):
        tile_copies[g].wait()

    @pl.loop(0, groups)
    def _(g):
        local_group(g)

    for piece, i, d in relays:
        do_relay(piece, i, d)
    for copy in state_copies:
        copy.wait()
    keep_copy.wait()
    for piece in range(pieces):
        for d in range(1 - half, half + 1):
            if d % 2 != 0:
                push(half, half - d, me + 1, piece, 0).wait_recv()

    ocean_c = coef_column(ocean_coef, block)
    ice_c = coef_column(ice_coef, block)
    land_c = coef_column(land_coef, block)

    def winds(d):
        row = d * 24
        u = mix[pl.ds(row, 8, 3), :]
        v = mix[pl.ds(row + 1, 8, 3), :]
        s = mix[pl.ds(row + 2, 8, 3), :]
        return jnp.sqrt(1.0 + u * u + v * v), s

    def back(d, flux):
        out = lax.dot_general(
            flux.astype(jnp.bfloat16),
            tiles[d].reshape(4 * block, block),
            (((1,), (1,)), ((), ())),
            preferred_element_type=jnp.float32,
        )
        for k in range(4):
            row = pl.multiple_of((4 * d + k) * 8, 8)
            terms[pl.ds(row, 8), :] = out[:, k * block : (k + 1) * block]

    def forward_group(first):
        for u in range(GROUP):
            d = first + u
            row = pl.multiple_of(d * 24, 24)
            mix[pl.ds(row, 24), :] = mix[pl.ds(row, 24), :] + product(d, 0)

    @pl.loop(0, ocean_blocks // GROUP)
    def _(g):
        forward_group(g * GROUP)
        for u in range(GROUP):
            d = g * GROUP + u
            lanes = pl.ds(pl.multiple_of(d * block, block), block)
            wind, scalar = winds(d)
            ice = li[pl.ds(d, 1), :].astype(jnp.float32) / 8.0
            flux = (1.0 - ice) * (ocean_c * wind * (scalar - so[:, lanes])) + ice * (
                ice_c * wind * (scalar - si[:, lanes])
            )
            ocn_v[:, lanes] = flux
            back(d, flux)

    @pl.loop(0, land_blocks // GROUP)
    def _(g):
        forward_group(ocean_blocks + g * GROUP)
        for u in range(GROUP):
            e = g * GROUP + u
            d = ocean_blocks + e
            lanes = pl.ds(pl.multiple_of(e * block, block), block)
            wind, scalar = winds(d)
            part = ll[pl.ds(e, 1), :].astype(jnp.float32) / 8.0
            flux = part * (land_c * wind * (scalar - sl[:, lanes]))
            lnd_v[:, lanes] = flux
            back(d, flux)

    ocn_copy = pltpu.make_async_copy(ocn_v, ocn_out, out_sem.at[0])
    lnd_copy = pltpu.make_async_copy(lnd_v, lnd_out, out_sem.at[1])
    ocn_copy.start()
    lnd_copy.start()

    rows = cells * blocks_here
    chosen = (
        lax.broadcasted_iota(jnp.int32, (rows, 4 * blocks), 0) == target[0:1, :]
    ).astype(jnp.float32).astype(jnp.bfloat16)
    for f in range(0, 8, 2):
        x = jnp.concatenate(
            [terms[pl.ds(f, 4 * blocks, 8), :], terms[pl.ds(f + 1, 4 * blocks, 8), :]], axis=1
        )
        high = x.astype(jnp.bfloat16)
        low = (x - high.astype(jnp.float32)).astype(jnp.bfloat16)
        total = jnp.dot(chosen, high, preferred_element_type=jnp.float32) + jnp.dot(
            chosen, low, preferred_element_type=jnp.float32
        )
        for w in range(cells):
            part = total[w * blocks_here : (w + 1) * blocks_here]
            for j in range(2):
                one = part[:, j * block : (j + 1) * block]
                if w == half:
                    own_sum[f + j] = one
                else:
                    outbox[w, f + j] = one.astype(jnp.bfloat16)

    def ship(w):
        return pltpu.make_async_remote_copy(
            src_ref=outbox.at[w],
            dst_ref=inbox.at[w],
            send_sem=back_send.at[w],
            recv_sem=back_recv.at[w],
            device_id=device(me + w - half),
            device_id_type=pl.DeviceIdType.MESH,
        )

    others = sorted((w for w in range(cells) if w != half), key=lambda w: -abs(w - half))
    shipped = [ship(w) for w in others]
    for copy in shipped:
        copy.start()
    for copy in shipped:
        copy.wait_recv()
    for f in range(8):
        value = own_sum[f]
        for w in others:
            value = value + inbox[w, f].astype(jnp.float32)
        final[pl.ds(f, blocks_here, 8), :] = value
    for b in range(blocks_here):
        atm_out[:, b * block : (b + 1) * block] = final[8 * b : 8 * b + 8, :]
    for copy in sends:
        copy.wait_send()
    for copy in shipped:
        copy.wait_send()
    ocn_copy.wait()
    lnd_copy.wait()


def per_device(
    sects,
    cells,
    atm_fields,
    ocn_state,
    ice_state,
    ice_level,
    lnd_state,
    lnd_level,
    ocn_map,
    ocn_local,
    ocn_tiles,
    lnd_map,
    lnd_local,
    lnd_tiles,
):
    fields, width = atm_fields.shape
    block = ocn_tiles.shape[2]
    fluxes = ocn_state.shape[0]
    blocks_here = width // block
    ocean_blocks, land_blocks = ocn_map.shape[0], lnd_map.shape[0]
    blocks = ocean_blocks + land_blocks
    count = sects * cells
    half = cells // 2
    me = lax.axis_index("sect") * cells + lax.axis_index("cell")
    mapped = jnp.concatenate([ocn_map, lnd_map], axis=0)
    local = jnp.concatenate([ocn_local, lnd_local], axis=0)
    span = count * blocks_here
    shifted = lax.rem(mapped + (span - (me - half) * blocks_here), span)
    picks = jnp.concatenate([shifted, local], axis=1).reshape(-1)
    targets = jnp.concatenate([shifted, local + half * blocks_here], axis=1).reshape(1, -1)
    pieces = 2
    evens = half
    any_spec = pl.BlockSpec(memory_space=pl.ANY)
    vmem_spec = pl.BlockSpec(memory_space=pltpu.VMEM)
    sizes = (sects, cells, ocean_blocks, land_blocks, blocks_here, block, pieces)
    f32, bf16 = jnp.float32, jnp.bfloat16
    sem = pltpu.SemaphoreType.DMA
    return pl.pallas_call(
        functools.partial(coupler_kernel, sizes),
        out_shape=(
            jax.ShapeDtypeStruct((fluxes, width), f32),
            jax.ShapeDtypeStruct(ocn_state.shape, f32),
            jax.ShapeDtypeStruct(lnd_state.shape, f32),
        ),
        in_specs=[pl.BlockSpec(memory_space=pltpu.SMEM), vmem_spec] + [any_spec] * 8,
        out_specs=(vmem_spec, any_spec, any_spec),
        scratch_shapes=[
            pltpu.VMEM((blocks_here, fields, block), bf16),
            pltpu.VMEM((cells * blocks_here, fields, block), bf16),
            pltpu.VMEM((blocks, 4, block, block), bf16),
            pltpu.VMEM(ocn_state.shape, f32),
            pltpu.VMEM(ice_state.shape, f32),
            pltpu.VMEM((ocean_blocks, block), jnp.int32),
            pltpu.VMEM(lnd_state.shape, f32),
            pltpu.VMEM((land_blocks, block), jnp.int32),
            pltpu.VMEM((blocks * fields, block), f32),
            pltpu.VMEM((blocks * 4 * fluxes, block), f32),
            pltpu.VMEM(ocn_state.shape, f32),
            pltpu.VMEM(lnd_state.shape, f32),
            pltpu.VMEM((cells, fluxes, blocks_here, block), bf16),
            pltpu.VMEM((cells, fluxes, blocks_here, block), bf16),
            pltpu.VMEM((fluxes, blocks_here, block), f32),
            pltpu.VMEM((blocks_here * fluxes, block), f32),
            sem((blocks_here,)),
            sem,
            sem((5,)),
            sem((blocks // GROUP,)),
            sem((2,)),
            sem((2 * evens, pieces)),
            sem((cells, pieces)),
            sem((cells,)),
            sem((cells,)),
        ],
        compiler_params=pltpu.CompilerParams(collective_id=0, has_side_effects=True),
    )(
        picks,
        targets,
        atm_fields,
        ocn_state,
        ice_state,
        ice_level.reshape(ocean_blocks, block),
        lnd_state,
        lnd_level.reshape(land_blocks, block),
        ocn_tiles,
        lnd_tiles,
    )


def solution(mesh):
    sects, cells = mesh.shape["sect"], mesh.shape["cell"]
    cut = ("sect", "cell")
    wide, flat = P(None, cut), P(cut)
    pair, quad = P(cut, None), P(cut, None, None, None)
    in_specs = (
        wide, wide, wide, flat, wide, flat, pair, pair, quad, pair, pair, quad,
    )
    return jax.shard_map(
        functools.partial(per_device, sects, cells),
        mesh=mesh,
        in_specs=in_specs,
        out_specs=(wide, wide, wide),
        check_vma=False,
    )
```

time: 211 us -> 58.5 us (0.28)
  waiting for transfers between devices: 105 us -> 0 us
  Pallas kernels: 0 us -> 49.8 us
  local copies, waits for them, and re-layouts: 43 us -> 6.26 us
  matrix products: 16.5 us -> 0 us
  other arithmetic: 16.2 us -> 1.58 us
  starting transfers between devices: 13.3 us -> 0 us
  blocking collectives: 13.2 us -> 0 us
    all_to_all x2 -> x0, waiting for transfers between devices: 59.7 us -> none  [the longest x1 33.8 us: per_device(): lax.all_to_all(relayed, 'cell', split_axis=0, concat_axis=0, tiled=True)]
    pallas_call x0 -> x1, Pallas kernels: none -> 49.8 us  [per_device(): pl.pallas_call(functools.partial(coupler_kernel, sizes), out_shape=(jax.S...]
    ppermute x6 -> x0, waiting for transfers between devices: 45 us -> none  [the longest x3 44.9 us: padded(): before = lax.ppermute(last, axis, up)]
    dot_general x7 -> x0, matrix products: 16.5 us -> none  [the longest x1 5.73 us: per_device(): jnp.einsum('bfd,bksd->bkfs', ocean_flux.astype(jnp.bfloat16), ocn_tiles,...]
    slice x11 -> x0, local copies, waits for them, and re-layouts: 14.3 us -> none  [the longest x2 2.6 us: bulk_flux(): return weights * wind_speed * (remapped[:, 2::3] - surface)]
    unnamed x1 -> x0, blocking collectives: 13.2 us -> none
    squeeze x4 -> x0, local copies, waits for them, and re-layouts: 8.52 us -> none  [the longest x3 7.43 us: per_device(): relayed = rimmed[0] + rimmed[2] + rimmed[4]]
    all_to_all x2 -> x0, starting transfers between devices: 8.1 us -> none  [the longest x1 4.48 us: per_device(): lax.all_to_all(relayed, 'cell', split_axis=0, concat_axis=0, tiled=True)]
  transfers between devices with their start and end apart: 8 -> 0, of which waited for: 5 -> 0; matrix products, arithmetic and copies ran while one was open for 7% -> 0% of each run, Pallas kernels for 0% -> 0%
where the time goes in v1:
time: 58.5 us; the launch traced here: 58.3 us
  Pallas kernels  49.8 us (85%)
  local copies, waits for them, and re-layouts  6.26 us (11%)
  other arithmetic  1.58 us (3%)
  between operations  0.65 us (1%)
    pallas_call x1, Pallas kernels, per_device(): pl.pallas_call(functools.partial(coupler_kernel, sizes), out_shape=(jax.S...  49.8 us
    unnamed x3, local copies, waits for them, and re-layouts  4.71 us

profile of v1, /device:TPU:0, one launch (start us, length us, event | category | flops | bytes accessed | tf_op | source)
XLA Modules:
  0.0 58.3 jit_solution(11955446181256874635)
XLA Ops:
  0.6 0.8 %compare_select_fusion = (s32[80,2]{0,1:T(2,128)S(1)}, s32[80,2]{0,1:T(2,128)S(1)}) fusion(s32[16,2]{0,1:T(2,128)} %param.21, s32[64,2]{0,1:T(2,128)} %param.18, s32[]{:T(128)S(6)} %sub.7, s32[16,2]{0,1:T(2,128)} %param.22, s32[64,2]{0,1:T(2,128)} %param.19), kind=kLoop, calls=%fused_computation.2 | loop fusion | flops 1600 | bytes 2564 | tf_op jit(solution)/shard_map/rem | solution.py:330
  1.4 0.8 %pad_add_fusion = (s32[80,4]{0,1:T(4,128)S(1)}, s32[80,4]{0,1:T(4,128)S(1)}) fusion(s32[80,2]{0,1:T(2,128)S(1)} %get-tuple-element.5, s32[80,2]{0,1:T(2,128)S(1)} %get-tuple-element.6, s32[16,2]{0,1:T(2,128)} %param.22, s32[64,2]{0,1:T(2,128)} %param.19), kind=kLoop, calls=%fused_computation | loop fusion | flops 960 | bytes 4480 | tf_op jit(solution)/shard_map/concatenate | solution.py:332
  2.2 0.1 copy.17
  2.3 0.7 %reshape.19.target = s32[1,320]{1,0:T(1,128)} reshape(s32[80,4]{1,0:T(8,128)S(1)} %copy.17) | data formatting | bytes 2560 | tf_op jit(solution)/shard_map/reshape | solution.py:332
  3.0 0.1 copy.16
  3.1 0.7 %reshape.18.pick = s32[320]{0:T(512)} reshape(s32[80,4]{1,0:T(8,128)S(1)} %copy.16) | data formatting | bytes 2560 | tf_op jit(solution)/shard_map/reshape | solution.py:331
  3.8 49.8 %shard_map.139 = (f32[8,4096]{1,0:T(8,128)}, f32[8,8192]{1,0:T(8,128)}, f32[8,2048]{1,0:T(8,128)}) custom-call(s32[320]{0:T(512)} %reshape.18.pick, s32[1,320]{1,0:T(1,128)} %reshape.19.target, bf16[24,4096]{1,0:T(8,128)(2,1)} %atm.1, f32[8,8192]{1,0:T(8,128)} %ocn_state.1, f32[8,8192]{1,0:T(8,128)} %ice_state.1, s32[64,128]{1,0:T(8,128)} %bitcast.2, ...), custom_call_target="tpu_custom_call" | custom-call | tf_op jit(solution)/shard_map/pallas_call | solution.py:340
  53.6 1.6 %copy.21 = f32[8,4096]{1,0:T(8,128)} copy(f32[8,4096]{1,0:T(8,128)} %get-tuple-element.10) | data formatting | bytes 262144
  55.1 1.7 %copy.22 = f32[8,8192]{1,0:T(8,128)} copy(f32[8,8192]{1,0:T(8,128)} %get-tuple-element.11) | data formatting | bytes 524288
  56.8 1.5 %copy.23 = f32[8,2048]{1,0:T(8,128)} copy(f32[8,2048]{1,0:T(8,128)} %get-tuple-element.12) | data formatting | bytes 131072

commit v2 on v1

v2 whole, which is shorter than its diff:
```python
import functools

import jax
import jax.numpy as jnp
from jax import lax
from jax.experimental import pallas as pl
from jax.experimental.pallas import tpu as pltpu
from jax.sharding import PartitionSpec as P

ocean_coef = (1.2, 0.9, 1.5, 0.7, 1.1, 1.3, 0.8, 1.0)
ice_coef = (0.5, 1.4, 0.6, 1.2, 0.9, 0.4, 1.6, 0.7)
land_coef = (0.8, 1.1, 0.6, 1.5, 0.7, 1.2, 1.0, 0.5)

GROUP = 8


def coef_column(coef, width):
    row = lax.broadcasted_iota(jnp.int32, (len(coef), width), 0)
    out = jnp.full((len(coef), width), coef[0], jnp.float32)
    for j in range(1, len(coef)):
        out = jnp.where(row == j, coef[j], out)
    return out


def coupler_kernel(
    sizes,
    ocn_map,
    ocn_local,
    lnd_map,
    lnd_local,
    atm,
    ocn_state,
    ice_state,
    ice_level,
    lnd_state,
    lnd_level,
    ocn_tiles,
    lnd_tiles,
    atm_out,
    ocn_out,
    lnd_out,
    pick_om,
    pick_ol,
    pick_lm,
    pick_ll,
    col_om,
    col_ol,
    col_lm,
    col_ll,
    own,
    held,
    tiles,
    so,
    si,
    li,
    sl,
    ll,
    mix,
    terms,
    ocn_v,
    lnd_v,
    sums,
    outbox,
    merge_in,
    merged,
    inbox,
    final,
    own_sem,
    keep_sem,
    state_sem,
    tile_sem,
    out_sem,
    send_sem,
    recv_sem,
    merge_send,
    merge_recv,
    back_send,
    back_recv,
):
    sects, cells, ocean_blocks, land_blocks, blocks_here, block, pieces = sizes
    count = sects * cells
    half = cells // 2
    rows = cells // 2
    blocks = ocean_blocks + land_blocks
    my_cell = lax.axis_index("cell")
    me = lax.axis_index("sect") * cells + my_cell
    my_row = lax.div(my_cell, 2)
    side = lax.rem(my_cell, 2)
    across = my_cell + 1 - 2 * side

    def device(number):
        number = lax.rem(number + 2 * count, count)
        return {"sect": lax.div(number, cells), "cell": lax.rem(number, cells)}

    def owner(j):
        return me - half + lax.rem(j - me + half + count, cells)

    def receiver(q, j):
        return q - half + 1 + lax.rem(j - q + half - 1 + 2 * count, cells)

    own_copies = []
    for b in range(blocks_here):
        src = atm.at[:, b * block : (b + 1) * block]
        copy = pltpu.make_async_copy(src, own.at[b], own_sem.at[b])
        copy.start()
        own_copies.append(copy)

    barrier = pltpu.get_barrier_semaphore()
    apart = sorted({1, 2, cells - 1, cells - 2} | set(range(2, half + 1, 2)))
    for d in apart:
        for number in (me + d, me - d):
            pl.semaphore_signal(
                barrier, inc=1, device_id=device(number), device_id_type=pl.DeviceIdType.MESH
            )

    small_copies = [
        pltpu.make_async_copy(src, dst, state_sem.at[i])
        for i, (src, dst) in enumerate(
            (
                (ocn_map, pick_om),
                (ocn_local, pick_ol),
                (lnd_map, pick_lm),
                (lnd_local, pick_ll),
                (ocn_map, col_om),
                (ocn_local, col_ol),
                (lnd_map, col_lm),
                (lnd_local, col_ll),
                (ocn_state, so),
                (ice_state, si),
                (ice_level, li),
                (lnd_state, sl),
                (lnd_level, ll),
            )
        )
    ]
    for copy in small_copies:
        copy.start()
    tile_copies = []
    for g in range(blocks // GROUP):
        first = g * GROUP
        if first < ocean_blocks:
            src = ocn_tiles.at[pl.ds(first, GROUP)]
        else:
            src = lnd_tiles.at[pl.ds(first - ocean_blocks, GROUP)]
        copy = pltpu.make_async_copy(src, tiles.at[pl.ds(first, GROUP)], tile_sem.at[g])
        copy.start()
        tile_copies.append(copy)

    for copy in own_copies:
        copy.wait()
    keep_copy = pltpu.make_async_copy(
        own, held.at[pl.ds(my_cell * blocks_here, blocks_here)], keep_sem
    )
    keep_copy.start()
    pl.semaphore_wait(barrier, 2 * len(apart))

    width = blocks_here // pieces

    def push(j, to_cell, piece, kind, mine):
        here = pl.ds(j * blocks_here + piece * width, width)
        src = own.at[pl.ds(piece * width, width)] if mine else held.at[here]
        return pltpu.make_async_remote_copy(
            src_ref=src,
            dst_ref=held.at[here],
            send_sem=send_sem.at[kind, lax.div(j, 2), piece],
            recv_sem=recv_sem.at[j, piece],
            device_id=device(receiver(owner(j), to_cell)),
            device_id_type=pl.DeviceIdType.MESH,
        )

    def send_up(j, piece, mine):
        return push(j, my_cell + 2, piece, 0, mine)

    def send_down(j, piece, mine):
        return push(j, my_cell - 2, piece, 1, mine)

    def send_across(j, piece, mine):
        return push(j, across, piece, 2, mine)

    for piece in range(pieces):

        @pl.when(my_row < rows - 1)
        def _():
            send_up(my_cell, piece, True).start()

        @pl.when(my_row > 0)
        def _():
            send_down(my_cell, piece, True).start()

        send_across(my_cell, piece, True).start()

    def dot_pair(source, d, refs, e, k):
        lhs = jnp.concatenate([source(refs[e, 0]), source(refs[e, 1])], axis=1)
        rhs = tiles[d, k : k + 2].reshape(2 * block, block)
        return jnp.dot(lhs, rhs, preferred_element_type=jnp.float32)

    span = cells * blocks_here

    def from_held(index):
        return held[lax.rem(index, span)]

    def from_own(index):
        return own[index]

    def local_part(refs, base, first):
        for u in range(GROUP):
            e = first + u
            d = base + e
            row = pl.multiple_of(d * 24, 24)
            mix[pl.ds(row, 24), :] = dot_pair(from_own, d, refs, e, 2)

    def step(k, piece):
        @pl.when(my_row - k >= 0)
        def _():
            j = my_cell - 2 * k
            send_across(j, piece, False).wait_recv()

            @pl.when(my_row < rows - 1)
            def _():
                send_up(j, piece, False).start()

            send_across(j, piece, False).start()

        @pl.when(my_row + k < rows)
        def _():
            j = my_cell + 2 * k
            send_across(j, piece, False).wait_recv()

            @pl.when(my_row > 0)
            def _():
                send_down(j, piece, False).start()

            send_across(j, piece, False).start()

    for copy in small_copies:
        copy.wait()
    for copy in tile_copies:
        copy.wait()

    @pl.loop(0, ocean_blocks // GROUP // 2)
    def _(g):
        local_part(pick_ol, 0, g * GROUP)

    step(1, 0)

    @pl.loop(ocean_blocks // GROUP // 2, ocean_blocks // GROUP)
    def _(g):
        local_part(pick_ol, 0, g * GROUP)

    @pl.loop(0, land_blocks // GROUP)
    def _(g):
        local_part(pick_ll, ocean_blocks, g * GROUP)

    for k in range(1, rows):
        for piece in range(pieces):
            if (k, piece) != (1, 0):
                step(k, piece)
    keep_copy.wait()

    lanes_of = lax.broadcasted_iota(jnp.int32, (1, span), 1)
    columns = []
    for k in range(4):
        if k < 2:
            pair = (lax.rem(col_om[...], span), lax.rem(col_lm[...], span))
        else:
            pair = (
                col_ol[...] + my_cell * blocks_here,
                col_ll[...] + my_cell * blocks_here,
            )
        columns += [part[:, k % 2 : k % 2 + 1] for part in pair]
    marks = jnp.concatenate(
        [(column == lanes_of).astype(jnp.float32) for column in columns], axis=0
    )
    chosen = marks.T.astype(jnp.bfloat16)

    for r in range(rows):
        for piece in range(pieces):
            send_across(2 * r + 1 - side, piece, False).wait_recv()

    ocean_c = coef_column(ocean_coef, block)
    ice_c = coef_column(ice_coef, block)
    land_c = coef_column(land_coef, block)

    def winds(d):
        row = d * 24
        u = mix[pl.ds(row, 8, 3), :]
        v = mix[pl.ds(row + 1, 8, 3), :]
        s = mix[pl.ds(row + 2, 8, 3), :]
        return jnp.sqrt(1.0 + u * u + v * v), s

    def back(d, flux):
        out = lax.dot_general(
            flux.astype(jnp.bfloat16),
            tiles[d].reshape(4 * block, block),
            (((1,), (1,)), ((), ())),
            preferred_element_type=jnp.float32,
        )
        for k in range(4):
            row = pl.multiple_of((k * blocks + d) * 8, 8)
            terms[pl.ds(row, 8), :] = out[:, k * block : (k + 1) * block]

    def forward_part(refs, base, first):
        for u in range(GROUP):
            e = first + u
            d = base + e
            row = pl.multiple_of(d * 24, 24)
            mix[pl.ds(row, 24), :] = mix[pl.ds(row, 24), :] + dot_pair(from_held, d, refs, e, 0)

    @pl.loop(0, ocean_blocks // GROUP)
    def _(g):
        forward_part(pick_om, 0, g * GROUP)
        for u in range(GROUP):
            d = g * GROUP + u
            lanes = pl.ds(pl.multiple_of(d * block, block), block)
            wind, scalar = winds(d)
            ice = li[pl.ds(d, 1), :].astype(jnp.float32) / 8.0
            flux = (1.0 - ice) * (ocean_c * wind * (scalar - so[:, lanes])) + ice * (
                ice_c * wind * (scalar - si[:, lanes])
            )
            ocn_v[:, lanes] = flux
            back(d, flux)

    @pl.loop(0, land_blocks // GROUP)
    def _(g):
        forward_part(pick_lm, ocean_blocks, g * GROUP)
        for u in range(GROUP):
            e = g * GROUP + u
            d = ocean_blocks + e
            lanes = pl.ds(pl.multiple_of(e * block, block), block)
            wind, scalar = winds(d)
            part = ll[pl.ds(e, 1), :].astype(jnp.float32) / 8.0
            flux = part * (land_c * wind * (scalar - sl[:, lanes]))
            lnd_v[:, lanes] = flux
            back(d, flux)

    ocn_copy = pltpu.make_async_copy(ocn_v, ocn_out, out_sem.at[0])
    lnd_copy = pltpu.make_async_copy(lnd_v, lnd_out, out_sem.at[1])
    ocn_copy.start()
    lnd_copy.start()

    for f in range(0, 8, 2):
        x = jnp.concatenate(
            [terms[pl.ds(f, 4 * blocks, 8), :], terms[pl.ds(f + 1, 4 * blocks, 8), :]], axis=1
        )
        high = x.astype(jnp.bfloat16)
        low = (x - high.astype(jnp.float32)).astype(jnp.bfloat16)
        total = jnp.dot(chosen, high, preferred_element_type=jnp.float32) + jnp.dot(
            chosen, low, preferred_element_type=jnp.float32
        )
        sums[f] = total[:, :block]
        sums[f + 1] = total[:, block:]

    def part_of(f, j):
        return sums[f, pl.ds(pl.multiple_of(j * blocks_here, blocks_here), blocks_here), :]

    def merge(r):
        j = 2 * r + 1 - side
        return pltpu.make_async_remote_copy(
            src_ref=outbox.at[r],
            dst_ref=merge_in.at[r],
            send_sem=merge_send.at[r],
            recv_sem=merge_recv.at[r],
            device_id=device(receiver(owner(j), across)),
            device_id_type=pl.DeviceIdType.MESH,
        )

    def ship(r):
        return pltpu.make_async_remote_copy(
            src_ref=merged.at[r],
            dst_ref=inbox.at[my_row],
            send_sem=back_send.at[r],
            recv_sem=back_recv.at[my_row],
            device_id=device(owner(2 * r + side)),
            device_id_type=pl.DeviceIdType.MESH,
        )

    def arrival(r):
        return pltpu.make_async_remote_copy(
            src_ref=merged.at[r],
            dst_ref=inbox.at[r],
            send_sem=back_send.at[r],
            recv_sem=back_recv.at[r],
            device_id=device(me + 1),
            device_id_type=pl.DeviceIdType.MESH,
        )

    order = [lax.rem(my_row + k, rows) for k in list(range(1, rows)) + [0]]
    for r in order:
        for f in range(8):
            outbox[r, f] = part_of(f, 2 * r + 1 - side).astype(jnp.bfloat16)
        merge(r).start()
    for r in order[:-1]:
        merge(r).wait_recv()
        for f in range(8):
            merged[r, f] = (
                part_of(f, 2 * r + side) + merge_in[r, f].astype(jnp.float32)
            ).astype(jnp.bfloat16)
        ship(r).start()
    merge(my_row).wait_recv()
    for r in order[:-1]:
        arrival(r).wait_recv()
    for f in range(8):
        value = part_of(f, my_cell) + merge_in[my_row, f].astype(jnp.float32)
        for r in order[:-1]:
            value = value + inbox[r, f].astype(jnp.float32)
        final[pl.ds(f, blocks_here, 8), :] = value
    for b in range(blocks_here):
        atm_out[:, b * block : (b + 1) * block] = final[8 * b : 8 * b + 8, :]
    for r in range(rows):
        j = 2 * r + side
        for piece in range(pieces):
            send_across(j, piece, False).wait_send()

            @pl.when((r <= my_row) & (my_row < rows - 1))
            def _():
                send_up(j, piece, False).wait_send()

            @pl.when((r >= my_row) & (my_row > 0))
            def _():
                send_down(j, piece, False).wait_send()

        merge(r).wait_send()
    for r in order[:-1]:
        ship(r).wait_send()
    ocn_copy.wait()
    lnd_copy.wait()


def finish_kernel(a, b, c, a_out, b_out, c_out):
    a_out[...] = a[...]
    b_out[...] = b[...]
    c_out[...] = c[...]


def per_device(
    sects,
    cells,
    atm_fields,
    ocn_state,
    ice_state,
    ice_level,
    lnd_state,
    lnd_level,
    ocn_map,
    ocn_local,
    ocn_tiles,
    lnd_map,
    lnd_local,
    lnd_tiles,
):
    fields, width = atm_fields.shape
    block = ocn_tiles.shape[2]
    fluxes = ocn_state.shape[0]
    blocks_here = width // block
    ocean_blocks, land_blocks = ocn_map.shape[0], lnd_map.shape[0]
    blocks = ocean_blocks + land_blocks
    pieces = 2
    rows = cells // 2
    any_spec = pl.BlockSpec(memory_space=pl.ANY)
    vmem_spec = pl.BlockSpec(memory_space=pltpu.VMEM)
    sizes = (sects, cells, ocean_blocks, land_blocks, blocks_here, block, pieces)
    f32, bf16, i32 = jnp.float32, jnp.bfloat16, jnp.int32
    sem = pltpu.SemaphoreType.DMA
    shapes = (
        jax.ShapeDtypeStruct((fluxes, width), f32),
        jax.ShapeDtypeStruct(ocn_state.shape, f32),
        jax.ShapeDtypeStruct(lnd_state.shape, f32),
    )
    maps = (ocn_map.shape, ocn_local.shape, lnd_map.shape, lnd_local.shape)
    results = pl.pallas_call(
        functools.partial(coupler_kernel, sizes),
        out_shape=shapes,
        in_specs=[any_spec] * 12,
        out_specs=(vmem_spec, any_spec, any_spec),
        scratch_shapes=[pltpu.SMEM(shape, i32) for shape in maps]
        + [pltpu.VMEM(shape, i32) for shape in maps]
        + [
            pltpu.VMEM((blocks_here, fields, block), bf16),
            pltpu.VMEM((cells * blocks_here, fields, block), bf16),
            pltpu.VMEM((blocks, 4, block, block), bf16),
            pltpu.VMEM(ocn_state.shape, f32),
            pltpu.VMEM(ice_state.shape, f32),
            pltpu.VMEM((ocean_blocks, block), i32),
            pltpu.VMEM(lnd_state.shape, f32),
            pltpu.VMEM((land_blocks, block), i32),
            pltpu.VMEM((blocks * fields, block), f32),
            pltpu.VMEM((blocks * 4 * fluxes, block), f32),
            pltpu.VMEM(ocn_state.shape, f32),
            pltpu.VMEM(lnd_state.shape, f32),
            pltpu.VMEM((fluxes, cells * blocks_here, block), f32),
            pltpu.VMEM((rows, fluxes, blocks_here, block), bf16),
            pltpu.VMEM((rows, fluxes, blocks_here, block), bf16),
            pltpu.VMEM((rows, fluxes, blocks_here, block), bf16),
            pltpu.VMEM((rows, fluxes, blocks_here, block), bf16),
            pltpu.VMEM((blocks_here * fluxes, block), f32),
            sem((blocks_here,)),
            sem,
            sem((13,)),
            sem((blocks // GROUP,)),
            sem((2,)),
            sem((3, rows, pieces)),
            sem((cells, pieces)),
            sem((rows,)),
            sem((rows,)),
            sem((rows,)),
            sem((rows,)),
        ],
        compiler_params=pltpu.CompilerParams(collective_id=0, has_side_effects=True),
    )(
        ocn_map,
        ocn_local,
        lnd_map,
        lnd_local,
        atm_fields,
        ocn_state,
        ice_state,
        ice_level.reshape(ocean_blocks, block),
        lnd_state,
        lnd_level.reshape(land_blocks, block),
        ocn_tiles,
        lnd_tiles,
    )
    return pl.pallas_call(
        finish_kernel,
        out_shape=shapes,
        in_specs=[vmem_spec] * 3,
        out_specs=(vmem_spec,) * 3,
    )(*results)


def solution(mesh):
    sects, cells = mesh.shape["sect"], mesh.shape["cell"]
    cut = ("sect", "cell")
    wide, flat = P(None, cut), P(cut)
    pair, quad = P(cut, None), P(cut, None, None, None)
    in_specs = (
        wide, wide, wide, flat, wide, flat, pair, pair, quad, pair, pair, quad,
    )
    return jax.shard_map(
        functools.partial(per_device, sects, cells),
        mesh=mesh,
        in_specs=in_specs,
        out_specs=(wide, wide, wide),
        check_vma=False,
    )
```

time: 58.5 us -> 50 us (0.85)
  Pallas kernels: 49.8 us -> 43.3 us
  other arithmetic: 1.58 us -> 0 us
  local copies, waits for them, and re-layouts: 6.26 us -> 5.46 us
    pallas_call x1 -> x2, Pallas kernels: 49.8 us -> 43.3 us  [the longest x1 41.5 us: per_device(): pl.pallas_call(functools.partial(coupler_kernel, sizes), out_shape=shapes...]
    reshape x2 -> x0, local copies, waits for them, and re-layouts: 1.35 us -> none  [the longest x1 0.68 us: per_device(): picks = jnp.concatenate([shifted, local], axis=1).reshape(-1)]
    rem x1 -> x0, other arithmetic: 0.81 us -> none  [per_device(): shifted = lax.rem(mapped + (span - (me - half) * blocks_here), span)]
    concatenate x1 -> x0, other arithmetic: 0.77 us -> none  [per_device(): jnp.concatenate([shifted, local + half * blocks_here], axis=1)]
    unnamed x3 -> x4, local copies, waits for them, and re-layouts: 4.71 us -> 5.46 us
where the time goes in v2:
time: 50 us; the launch traced here: 49.4 us
  Pallas kernels  43.3 us (87%)
  local copies, waits for them, and re-layouts  5.46 us (11%)
  between operations  0.64 us (1%)
    pallas_call x1, Pallas kernels, per_device(): pl.pallas_call(functools.partial(coupler_kernel, sizes), out_shape=shapes...  41.5 us
    unnamed x4, local copies, waits for them, and re-layouts  5.46 us
    pallas_call x1, Pallas kernels, per_device(): pl.pallas_call(finish_kernel, out_shape=shapes, in_specs=[vmem_spec] * 3,...  1.76 us

profile of v2, /device:TPU:0, one launch (start us, length us, event | category | flops | bytes accessed | tf_op | source)
XLA Modules:
  0.0 49.4 jit_solution(15458722758933041411)
XLA Ops:
  0.6 1.4 %copy.17.lnd_map = s32[16,2]{1,0:T(8,128)} copy(s32[16,2]{0,1:T(2,128)} %param.21) | data formatting | bytes 256 | tf_op args[9]
  2.0 1.3 %copy.18.lnd_local = s32[16,2]{1,0:T(8,128)} copy(s32[16,2]{0,1:T(2,128)} %param.22) | data formatting | bytes 256 | tf_op args[10]
  3.3 1.4 %copy.15.ocn_map = s32[64,2]{1,0:T(8,128)} copy(s32[64,2]{0,1:T(2,128)} %param.18) | data formatting | bytes 1024 | tf_op args[6]
  4.7 1.4 %copy.16.ocn_local = s32[64,2]{1,0:T(8,128)} copy(s32[64,2]{0,1:T(2,128)} %param.19) | data formatting | bytes 1024 | tf_op args[7]
  6.1 41.5 %shard_map.139 = (f32[8,4096]{1,0:T(8,128)}, f32[8,8192]{1,0:T(8,128)}, f32[8,2048]{1,0:T(8,128)}) custom-call(s32[64,2]{1,0:T(8,128)} %copy.15.ocn_map, s32[64,2]{1,0:T(8,128)} %copy.16.ocn_local, s32[16,2]{1,0:T(8,128)} %copy.17.lnd_map, s32[16,2]{1,0:T(8,128)} %copy.18.lnd_local, bf16[24,4096]{1,0:T(8,128)(2,1)} %atm.1, f32[8,8192]{1,0:T(8,128)} %ocn_state.1, ...), custom_call_target="tpu_custom_call" | custom-call | tf_op jit(solution)/shard_map/pallas_call | solution.py:470
  47.6 1.8 %shard_map.140 = (f32[8,4096]{1,0:T(8,128)}, f32[8,8192]{1,0:T(8,128)}, f32[8,2048]{1,0:T(8,128)}) custom-call(f32[8,4096]{1,0:T(8,128)} %get-tuple-element.6.a, f32[8,8192]{1,0:T(8,128)} %get-tuple-element.7.b, f32[8,2048]{1,0:T(8,128)} %get-tuple-element.8.c), custom_call_target="tpu_custom_call" | custom-call | tf_op jit(solution)/shard_map/pallas_call | solution.py:523

commit v3 on v2

--- a/solution.py
+++ b/solution.py
@@ -12,6 +12,7 @@
 land_coef = (0.8, 1.1, 0.6, 1.5, 0.7, 1.2, 1.0, 0.5)
 
 GROUP = 8
+DEPTH = 4
 
 
 def coef_column(coef, width):
@@ -190,7 +191,7 @@
         send_across(my_cell, piece, True).start()
 
     def dot_pair(source, d, refs, e, k):
-        lhs = jnp.concatenate([source(refs[e, 0]), source(refs[e, 1])], axis=1)
+        lhs = jnp.concatenate([source(refs[0, e]), source(refs[1, e])], axis=1)
         rhs = tiles[d, k : k + 2].reshape(2 * block, block)
         return jnp.dot(lhs, rhs, preferred_element_type=jnp.float32)
 
@@ -257,21 +258,19 @@
                 step(k, piece)
     keep_copy.wait()
 
-    lanes_of = lax.broadcasted_iota(jnp.int32, (1, span), 1)
-    columns = []
+    parts = []
     for k in range(4):
-        if k < 2:
-            pair = (lax.rem(col_om[...], span), lax.rem(col_lm[...], span))
-        else:
-            pair = (
-                col_ol[...] + my_cell * blocks_here,
-                col_ll[...] + my_cell * blocks_here,
-            )
-        columns += [part[:, k % 2 : k % 2 + 1] for part in pair]
-    marks = jnp.concatenate(
-        [(column == lanes_of).astype(jnp.float32) for column in columns], axis=0
+        for mapped, local in ((col_om, col_ol), (col_lm, col_ll)):
+            if k < 2:
+                parts.append(lax.rem(mapped[k : k + 1, :], span))
+            else:
+                parts.append(local[k - 2 : k - 1, :] + my_cell * blocks_here)
+    target = jnp.concatenate(parts, axis=1)
+    chosen = (
+        (lax.broadcasted_iota(jnp.int32, (span, 4 * blocks), 0) == target)
+        .astype(jnp.float32)
+        .astype(jnp.bfloat16)
     )
-    chosen = marks.T.astype(jnp.bfloat16)
 
     for r in range(rows):
         for piece in range(pieces):
@@ -385,9 +384,11 @@
         )
 
     order = [lax.rem(my_row + k, rows) for k in list(range(1, rows)) + [0]]
-    for r in order:
+    for i, r in enumerate(order):
         for f in range(8):
             outbox[r, f] = part_of(f, 2 * r + 1 - side).astype(jnp.bfloat16)
+        if i >= DEPTH:
+            merge(order[i - DEPTH]).wait_send()
         merge(r).start()
     for r in order[:-1]:
         merge(r).wait_recv()
@@ -419,6 +420,7 @@
             def _():
                 send_down(j, piece, False).wait_send()
 
+    for r in order[-DEPTH:]:
         merge(r).wait_send()
     for r in order[:-1]:
         ship(r).wait_send()
@@ -466,7 +468,7 @@
         jax.ShapeDtypeStruct(ocn_state.shape, f32),
         jax.ShapeDtypeStruct(lnd_state.shape, f32),
     )
-    maps = (ocn_map.shape, ocn_local.shape, lnd_map.shape, lnd_local.shape)
+    maps = [x.shape[::-1] for x in (ocn_map, ocn_local, lnd_map, lnd_local)]
     results = pl.pallas_call(
         functools.partial(coupler_kernel, sizes),
         out_shape=shapes,
@@ -507,10 +509,10 @@
         ],
         compiler_params=pltpu.CompilerParams(collective_id=0, has_side_effects=True),
     )(
-        ocn_map,
-        ocn_local,
-        lnd_map,
-        lnd_local,
+        ocn_map.T,
+        ocn_local.T,
+        lnd_map.T,
+        lnd_local.T,
         atm_fields,
         ocn_state,
         ice_state,

time: 50 us -> 44.6 us (0.89)
  local copies, waits for them, and re-layouts: 5.46 us -> 0 us
    unnamed x4 -> x0, local copies, waits for them, and re-layouts: 5.46 us -> none
where the time goes in v3:
time: 44.6 us; the launch traced here: 44 us
  Pallas kernels  43.4 us (97%)
  between operations  0.64 us (1%)
    pallas_call x1, Pallas kernels, per_device(): pl.pallas_call(functools.partial(coupler_kernel, sizes), out_shape=shapes...  41.6 us
    pallas_call x1, Pallas kernels, per_device(): pl.pallas_call(finish_kernel, out_shape=shapes, in_specs=[vmem_spec] * 3,...  1.76 us

profile of v3, /device:TPU:0, one launch (start us, length us, event | category | flops | bytes accessed | tf_op | source)
XLA Modules:
  0.0 44.0 jit_solution(1049063635445917211)
XLA Ops:
  0.6 41.6 %shard_map.139 = (f32[8,4096]{1,0:T(8,128)}, f32[8,8192]{1,0:T(8,128)}, f32[8,2048]{1,0:T(8,128)}) custom-call(s32[2,64]{1,0:T(2,128)} %bitcast.8, s32[2,64]{1,0:T(2,128)} %bitcast.9, s32[2,16]{1,0:T(2,128)} %bitcast.10, s32[2,16]{1,0:T(2,128)} %bitcast.11, bf16[24,4096]{1,0:T(8,128)(2,1)} %atm.1, f32[8,8192]{1,0:T(8,128)} %ocn_state.1, ...), custom_call_target="tpu_custom_call" | custom-call | tf_op jit(solution)/shard_map/pallas_call | solution.py:472
  42.2 1.8 %shard_map.140 = (f32[8,4096]{1,0:T(8,128)}, f32[8,8192]{1,0:T(8,128)}, f32[8,2048]{1,0:T(8,128)}) custom-call(f32[8,4096]{1,0:T(8,128)} %get-tuple-element.6.a, f32[8,8192]{1,0:T(8,128)} %get-tuple-element.7.b, f32[8,2048]{1,0:T(8,128)} %get-tuple-element.8.c), custom_call_target="tpu_custom_call" | custom-call | tf_op jit(solution)/shard_map/pallas_call | solution.py:525
